TPU v7x, 32 devices: a whole 2x2x4 slice. The times are simulated.
32 devices in a mesh: rep: 4 (over x, core), fsdp: 2 (over y), cp: 4 (over z).
Axes of the slice: x: 2, y: 2, z: 4, core: 2. Of those that a mesh axis runs over, the one named last changes fastest.
Arguments:
- tokens: bfloat16 [8, 512, 1024], P(('rep', 'fsdp'), 'cp'), may hold values from -6 to 6
- segments: int32 [8, 512], P(('rep', 'fsdp'), 'cp'), may hold values from 0 to 15, never falling along the last dimension, each value on 1 to 64 neighbouring positions
- cotangent: bfloat16 [8, 512, 1024], P(('rep', 'fsdp'), 'cp'), may hold values from -6 to 6
- w_qkv: bfloat16 [1024, 3072], P(('fsdp', 'cp')), may hold values from -8 to 8
- w_attn: bfloat16 [1024, 1024], P(('fsdp', 'cp')), may hold values from -0.75 to 0.75
- w_in: bfloat16 [1024, 5248], P(('fsdp', 'cp')), may hold values from -0.1875 to 0.1875
- w_mlp: bfloat16 [2624, 1024], P(None, ('fsdp', 'cp')), may hold values from -0.125 to 0.125
- gain_attn: bfloat16 [1024], P(('fsdp', 'cp')), may hold values from 0.3984375 to 1.59375
- gain_mlp: bfloat16 [1024], P(('fsdp', 'cp')), may hold values from 0.3984375 to 1.59375
Outputs:
- output: bfloat16 [8, 512, 1024], P(('rep', 'fsdp'), 'cp')
- grad_tokens: bfloat16 [8, 512, 1024], P(('rep', 'fsdp'), 'cp')
- grad_qkv: float32 [1024, 3072], P(('fsdp', 'cp'))
- grad_attn: float32 [1024, 1024], P(('fsdp', 'cp'))
- grad_in: float32 [1024, 5248], P(('fsdp', 'cp'))
- grad_mlp: float32 [2624, 1024], P(None, ('fsdp', 'cp'))
- grad_gain_attn: float32 [1024], P(('fsdp', 'cp'))
- grad_gain_mlp: float32 [1024], P(('fsdp', 'cp'))
Inputs may be any that keep to these rules, and one draw needn't show every extreme that they name: `segments`: along each sequence segment ids never fall; each document holds 1 to 64 tokens, and one holds exactly 64.
All inputs are finite; a program needn't handle non-finite values.
Results may differ from a plain program's by a relative error of at most 0.012.
Values may be sent and summed in bfloat16 or wider, within the bound.
A program may use at most 192 MiB of HBM per device.

v0:
```python
import math

import jax
import jax.numpy as jnp
from jax import lax
from jax.sharding import PartitionSpec as P

HEADS = 16


EPS = 1e-05
THETA = 160000.0
NEG = -1e30
GROUP = 4


def from_behind(value, axis, steps):
    count = lax.axis_size(axis)
    initial, last = (max(0, -steps), min(count, count - steps))
    return lax.ppermute(value, axis, [(source, source + steps) for source in range(initial, last)])


def layer_norm(values):
    mean = jnp.mean(values, -1, keepdims=True)
    centred = values - mean
    var = jnp.mean(centred * centred, -1, keepdims=True)
    rstd = lax.rsqrt(var + EPS)
    return (centred * rstd, rstd)


def norm_back(grad_norm, normed, rstd):
    mean_grad = jnp.mean(grad_norm, -1, keepdims=True)
    mean_dot = jnp.mean(grad_norm * normed, -1, keepdims=True)
    return (grad_norm - mean_grad - normed * mean_dot) * rstd


def rope_tables(positions, half):
    index = jnp.arange(half, dtype=jnp.float32)
    inverse = jnp.exp(-(2.0 * index / (2.0 * half)) * math.log(THETA))
    angle = positions[:, None] * inverse[None, :]
    return (jnp.cos(angle)[:, None, :], jnp.sin(angle)[:, None, :])


def rotate(values, cosine, sine):
    half = cosine.shape[-1]
    first, second = (values[..., :half], values[..., half:])
    return jnp.concatenate([first * cosine - second * sine, second * cosine + first * sine], -1)


def unrotate(values, cosine, sine):
    half = cosine.shape[-1]
    first, second = (values[..., :half], values[..., half:])
    return jnp.concatenate([first * cosine + second * sine, second * cosine - first * sine], -1)


def gelu_parts(values):
    cdf = 0.5 * (1.0 + jax.scipy.special.erf(values / math.sqrt(2.0)))
    slope = cdf + values * jnp.exp(-0.5 * values * values) / math.sqrt(2.0 * math.pi)
    return (values * cdf, slope)


def split_groups(values):
    rows, heads, width = values.shape
    return values.reshape(rows, heads // GROUP, GROUP, width).transpose(1, 0, 2, 3)


def join_groups(values):
    groups, rows, heads, width = values.shape
    return values.transpose(1, 0, 2, 3).reshape(rows, groups * heads, width)


def scores(query, keys, same):
    scale = 1.0 / math.sqrt(query.shape[-1])
    raw = jnp.einsum("nhe,lhe->hnl", query, keys, preferred_element_type=jnp.float32) * scale
    return jnp.where(same[None], raw, NEG)


def attend(query, keys, values, same):

    def one(group):
        qg, kg, vg = group
        logits = scores(qg, kg, same)
        top = jnp.max(logits, -1, keepdims=True)
        lse = top + jnp.log(jnp.sum(jnp.exp(logits - top), -1, keepdims=True))
        probs = jnp.exp(logits - lse).astype(jnp.bfloat16)
        mixed = jnp.einsum("hnl,lhe->nhe", probs, vg, preferred_element_type=jnp.float32)
        return (mixed, lse)

    mixed, lse = lax.map(one, (split_groups(query), split_groups(keys), split_groups(values)))
    return (join_groups(mixed), lse)


def attend_back(query, keys, values, mixed, grad_mixed, lse, same):
    scale = 1.0 / math.sqrt(query.shape[-1])

    def one(group):
        qg, kg, vg, og, dog, lg = group
        logits = scores(qg, kg, same)
        probs = jnp.exp(logits - lg)
        probs_b = probs.astype(jnp.bfloat16)
        grad_v = jnp.einsum("hnl,nhe->lhe", probs_b, dog, preferred_element_type=jnp.float32)
        grad_p = jnp.einsum("nhe,lhe->hnl", dog, vg, preferred_element_type=jnp.float32)
        delta = jnp.sum(dog.astype(jnp.float32) * og.astype(jnp.float32), -1).transpose(1, 0)
        grad_s = (probs * (grad_p - delta[..., None])).astype(jnp.bfloat16)
        grad_q = jnp.einsum("hnl,lhe->nhe", grad_s, kg, preferred_element_type=jnp.float32) * scale
        grad_k = jnp.einsum("hnl,nhe->lhe", grad_s, qg, preferred_element_type=jnp.float32) * scale
        return (grad_q, grad_k, grad_v)

    parts = (
        split_groups(query),
        split_groups(keys),
        split_groups(values),
        split_groups(mixed),
        split_groups(grad_mixed),
        lse,
    )
    grad_q, grad_k, grad_v = lax.map(one, parts)
    return (join_groups(grad_q), join_groups(grad_k), join_groups(grad_v))


def fetch_near(keys_local, values_local, reach):
    key_parts = []
    value_parts = []
    for offset in range(-reach, reach + 1):
        if offset == 0:
            key_parts.append(keys_local)
            value_parts.append(values_local)
        else:
            got_k, got_v = from_behind((keys_local, values_local), "cp", -offset)
            key_parts.append(got_k)
            value_parts.append(got_v)
    return (jnp.concatenate(key_parts, 0), jnp.concatenate(value_parts, 0))


def return_near(grad_keys, grad_values, reach, rows):
    own_k = grad_keys[reach * rows : (reach + 1) * rows]
    own_v = grad_values[reach * rows : (reach + 1) * rows]
    for offset in range(-reach, reach + 1):
        if offset != 0:
            lower = (reach + offset) * rows
            got_k, got_v = (
                from_behind(
                    grad_keys[lower : lower + rows].astype(jnp.bfloat16), "cp", offset
                ).astype(jnp.float32),
                from_behind(
                    grad_values[lower : lower + rows].astype(jnp.bfloat16), "cp", offset
                ).astype(jnp.float32),
            )
            own_k = own_k + got_k
            own_v = own_v + got_v
    return (own_k, own_v)


def shards(tokens, segments, cotangent, w_qkv, w_attn, w_in, w_mlp, gain_attn, gain_mlp):
    local_tokens = tokens[0]
    local_segments = segments[0]
    local_cotangent = cotangent[0]
    rows, width = local_tokens.shape
    heads = HEADS
    size = width // heads
    blocks = lax.axis_size("cp")
    position = lax.axis_index("cp")
    full = (
        lax.all_gather(w_qkv, ("fsdp", "cp"), axis=0, tiled=True),
        lax.all_gather(w_attn, ("fsdp", "cp"), axis=0, tiled=True),
        lax.all_gather(w_in, ("fsdp", "cp"), axis=0, tiled=True),
        lax.all_gather(w_mlp, ("fsdp", "cp"), axis=1, tiled=True),
        lax.all_gather(gain_attn, ("fsdp", "cp"), axis=0, tiled=True),
        lax.all_gather(gain_mlp, ("fsdp", "cp"), axis=0, tiled=True),
    )
    f_qkv, f_attn, f_in, f_mlp, f_gone, f_gtwo = full
    hidden = f_mlp.shape[0]
    key_segments = lax.all_gather(local_segments, "cp", axis=0, tiled=True)
    index = position * rows + jnp.arange(rows, dtype=jnp.int32)
    start = jnp.sum((key_segments[None, :] < local_segments[:, None]).astype(jnp.int32), 1)
    cosine, sine = rope_tables((index - start).astype(jnp.float32), size // 2)
    doc_most = rows * blocks // 8
    reach = min(blocks - 1, (doc_most - 1) // rows + 1)
    g_one = f_gone.astype(jnp.float32)
    g_two = f_gtwo.astype(jnp.float32)
    inputs = local_tokens.astype(jnp.float32)
    n_one, r_one = layer_norm(inputs)
    h_one = (n_one * g_one).astype(jnp.bfloat16)
    qkv = jnp.dot(h_one, f_qkv, preferred_element_type=jnp.float32).reshape(rows, 3, heads, size)
    query = rotate(qkv[:, 0], cosine, sine).astype(jnp.bfloat16)
    keys_local = rotate(qkv[:, 1], cosine, sine).astype(jnp.bfloat16).reshape(rows, width)
    values_local = qkv[:, 2].astype(jnp.bfloat16).reshape(rows, width)
    offsets = jnp.arange(-reach, reach + 1, dtype=jnp.int32)
    block_ids = position + offsets
    inside = (block_ids >= 0) & (block_ids < blocks)
    clamped = jnp.clip(block_ids, 0, blocks - 1)
    window_segments = jnp.take(key_segments.reshape(blocks, rows), clamped, axis=0).reshape(-1)
    window_inside = jnp.repeat(inside, rows)
    same = (local_segments[:, None] == window_segments[None, :]) & window_inside[None, :]
    keys_flat, values_flat = fetch_near(keys_local, values_local, reach)
    span = keys_flat.shape[0]
    keys = keys_flat.reshape(span, heads, size)
    values = values_flat.reshape(span, heads, size)
    mixed, lse = attend(query, keys, values, same)
    mixed_b = mixed.astype(jnp.bfloat16)
    flat_mixed = mixed_b.reshape(rows, width)
    x_two = inputs + jnp.dot(flat_mixed, f_attn, preferred_element_type=jnp.float32)
    n_two, r_two = layer_norm(x_two)
    h_two = (n_two * g_two).astype(jnp.bfloat16)
    proj = jnp.dot(h_two, f_in, preferred_element_type=jnp.float32)
    act_in, gate = (proj[:, :hidden], proj[:, hidden:])
    act, slope = gelu_parts(act_in)
    inner = (act * gate).astype(jnp.bfloat16)
    output = (x_two + jnp.dot(inner, f_mlp, preferred_element_type=jnp.float32)).astype(
        jnp.bfloat16
    )
    back = (
        lax.all_gather(w_qkv, ("fsdp", "cp"), axis=0, tiled=True),
        lax.all_gather(w_attn, ("fsdp", "cp"), axis=0, tiled=True),
        lax.all_gather(w_in, ("fsdp", "cp"), axis=0, tiled=True),
        lax.all_gather(w_mlp, ("fsdp", "cp"), axis=1, tiled=True),
        lax.all_gather(gain_attn, ("fsdp", "cp"), axis=0, tiled=True),
        lax.all_gather(gain_mlp, ("fsdp", "cp"), axis=0, tiled=True),
    )
    b_qkv, b_attn, b_in, b_mlp, b_gone, b_gtwo = back
    bg_one = b_gone.astype(jnp.float32)
    bg_two = b_gtwo.astype(jnp.float32)
    grad_out = local_cotangent.astype(jnp.float32)
    grad_mlp = jnp.dot(inner.T, local_cotangent, preferred_element_type=jnp.float32)
    grad_inner = jnp.dot(local_cotangent, b_mlp.T, preferred_element_type=jnp.float32)
    grad_proj = jnp.concatenate([grad_inner * gate * slope, grad_inner * act], -1).astype(
        jnp.bfloat16
    )
    grad_in = jnp.dot(h_two.T, grad_proj, preferred_element_type=jnp.float32)
    grad_h_two = jnp.dot(grad_proj, b_in.T, preferred_element_type=jnp.float32)
    grad_g_two = jnp.sum(grad_h_two * n_two, 0)
    grad_x_two = grad_out + norm_back(grad_h_two * bg_two, n_two, r_two)
    grad_a = grad_x_two.astype(jnp.bfloat16)
    grad_attn = jnp.dot(flat_mixed.T, grad_a, preferred_element_type=jnp.float32)
    grad_mixed = jnp.dot(grad_a, b_attn.T, preferred_element_type=jnp.float32).astype(jnp.bfloat16)
    back_keys, back_values = (keys, values)
    grad_q, grad_k_all, grad_v_all = attend_back(
        query, back_keys, back_values, mixed_b, grad_mixed.reshape(rows, heads, size), lse, same
    )
    grad_k_own, grad_v_own = return_near(
        grad_k_all.reshape(span, width), grad_v_all.reshape(span, width), reach, rows
    )
    grad_q = unrotate(grad_q, cosine, sine)
    grad_k = unrotate(grad_k_own.reshape(rows, heads, size), cosine, sine)
    grad_v = grad_v_own.reshape(rows, heads, size)
    grad_qkv_rows = (
        jnp.stack([grad_q, grad_k, grad_v], 1).reshape(rows, 3 * width).astype(jnp.bfloat16)
    )
    grad_qkv = jnp.dot(h_one.T, grad_qkv_rows, preferred_element_type=jnp.float32)
    grad_h_one = jnp.dot(grad_qkv_rows, b_qkv.T, preferred_element_type=jnp.float32)
    grad_g_one = jnp.sum(grad_h_one * n_one, 0)
    grad_tokens = (grad_x_two + norm_back(grad_h_one * bg_one, n_one, r_one)).astype(jnp.bfloat16)
    owned = (
        lax.psum_scatter(grad_qkv, ("fsdp", "cp"), scatter_dimension=0, tiled=True),
        lax.psum_scatter(grad_attn, ("fsdp", "cp"), scatter_dimension=0, tiled=True),
        lax.psum_scatter(grad_in, ("fsdp", "cp"), scatter_dimension=0, tiled=True),
        lax.psum_scatter(grad_mlp, ("fsdp", "cp"), scatter_dimension=1, tiled=True),
        lax.psum_scatter(grad_g_one, ("fsdp", "cp"), scatter_dimension=0, tiled=True),
        lax.psum_scatter(grad_g_two, ("fsdp", "cp"), scatter_dimension=0, tiled=True),
    )
    summed = lax.psum((owned[0], owned[1], owned[2], owned[3], owned[4], owned[5]), "rep")
    return (
        output[None],
        grad_tokens[None],
        summed[0],
        summed[1],
        summed[2],
        summed[3],
        summed[4],
        summed[5],
    )


def solution(mesh):
    in_specs = (
        P(("rep", "fsdp"), "cp", None),
        P(("rep", "fsdp"), "cp"),
        P(("rep", "fsdp"), "cp", None),
        P(("fsdp", "cp"), None),
        P(("fsdp", "cp"), None),
        P(("fsdp", "cp"), None),
        P(None, ("fsdp", "cp")),
        P(("fsdp", "cp")),
        P(("fsdp", "cp")),
    )
    out_specs = (
        P(("rep", "fsdp"), "cp", None),
        P(("rep", "fsdp"), "cp", None),
        P(("fsdp", "cp"), None),
        P(("fsdp", "cp"), None),
        P(("fsdp", "cp"), None),
        P(None, ("fsdp", "cp")),
        P(("fsdp", "cp")),
        P(("fsdp", "cp")),
    )
    return jax.shard_map(shards, mesh=mesh, in_specs=in_specs, out_specs=out_specs, check_vma=False)
```

profile of v0, /device:TPU:0, one launch (start us, length us, event | category | flops | bytes accessed | tf_op | source)
XLA Modules:
  0.0 1393.1 jit_solution(7403454981330167489)
XLA Ops:
  10.1 22.7 %all-gather.1 = bf16[8,1,128]{2,1,0:T(2,128)(2,1)S(1)} all-gather(bf16[1,1,128]{2,1,0:T(2,128)(2,1)S(1)} %bitcast.305), channel_id=1, replica_groups=mesh['rep'=4,'fsdp'=2,'cp'=4] {'fsdp','cp'}, dimensions={0}, use_global_device_ids=true | all-gather | bytes 2304 | tf_op jit(solution)/shard_map/all_gather | solution.py:168
  32.8 7.9 all-gather
  40.7 18.7 %all-gather.2 = bf16[8,1,128]{2,1,0:T(2,128)(2,1)S(1)} all-gather(bf16[1,1,128]{2,1,0:T(2,128)(2,1)S(1)} %bitcast.306), channel_id=1, replica_groups=mesh['rep'=4,'fsdp'=2,'cp'=4] {'fsdp','cp'}, dimensions={0}, use_global_device_ids=true | all-gather | bytes 2304 | tf_op jit(solution)/shard_map/all_gather | solution.py:169
  60.9 50.7 %all-gather.8.cloned.1.call-done = bf16[1024,3072]{1,0:T(8,128)(2,1)} async-done(((bf16[128,3072]{1,0:T(8,128)(2,1)}), bf16[1024,3072]{1,0:T(8,128)(2,1)}) %all-gather.8.cloned.1.call-update) | async-done | bytes 6291472 | tf_op jit(solution)/shard_map/all_gather | solution.py:164
  111.7 8.7 copy.29
  120.3 4.8 fusion.76
  126.4 4.6 collective-permute-start
  132.5 4.6 collective-permute-start.2
  139.0 6.8 collective-permute-done.3
  145.9 5.0 while.30
  150.9 12.8 all-gather.10.cloned.1.call-done
  166.1 152.0 %all-gather.12.cloned.1.call-done = bf16[1024,5248]{1,0:T(8,128)(2,1)} async-done(((bf16[128,5248]{1,0:T(8,128)(2,1)}), bf16[1024,5248]{1,0:T(8,128)(2,1)}) %all-gather.12.cloned.1.call-update) | async-done | bytes 10747920 | tf_op jit(solution)/shard_map/all_gather | solution.py:166
  318.1 7.3 fusion.92
  325.4 81.2 %all-gather.14.cloned.1.call-done = bf16[2624,1024]{1,0:T(8,128)(2,1)} async-done(((bf16[2624,128]{1,0:T(8,128)(2,1)}), bf16[2624,1024]{1,0:T(8,128)(2,1)}) %all-gather.14.cloned.1.call-update) | async-done | bytes 5373968 | tf_op jit(solution)/shard_map/all_gather | solution.py:167
  406.6 5.3 fusion.52
  411.9 8.2 multiply_reduce_fusion
  423.4 7.6 fusion.78
  431.1 3.1 convolution_convert_fusion
  435.3 21.7 %while.31 = (s32[]{:T(128)}, f32[4,128,4,64]{1,3,2,0:T(8,128)}, f32[4,384,4,64]{1,3,2,0:T(8,128)}, f32[4,384,4,64]{1,3,2,0:T(8,128)}, bf16[4,384,4,64]{1,3,2,0:T...) while((s32[]{:T(128)}, f32[4,128,4,64]{1,3,2,0:T(8,128)}, ...), condition=%wide.region_13.14_spmd.clone.clone, body=%wide.region_11.13_spmd.clone.sunk.clone | while | flops 127565312 | bytes 5555725 | solution.py:117
  462.1 5.1 collective-permute-start.7
  470.5 2.9 collective-permute-done.7
  476.9 6.4 fusion.82
  484.7 9.2 fusion.55
  493.9 16.0 %reduce-scatter.7.cloned.1.call-done = f32[128,1024]{1,0:T(8,128)} async-done(((f32[1024,1024]{1,0:T(8,128)}), f32[128,1024]{1,0:T(8,128)}) %reduce-scatter.7.cloned.1.call-update) | async-done | bytes 524304 | tf_op jit(solution)/shard_map/reduce_scatter | solution.py:255
  509.9 185.4 %reduce-scatter.11.cloned.1.call-done = f32[2624,128]{1,0:T(8,128)} async-done(((f32[2624,1024]{1,0:T(8,128)}), f32[2624,128]{1,0:T(8,128)}) %reduce-scatter.11.cloned.1.call-update) | async-done | bytes 1343504 | tf_op jit(solution)/shard_map/reduce_scatter | solution.py:257
  695.4 210.2 %reduce-scatter.5.cloned.1.call-done = f32[128,3072]{1,0:T(8,128)} async-done(((f32[1024,3072]{1,0:T(8,128)}), f32[128,3072]{1,0:T(8,128)}) %reduce-scatter.5.cloned.1.call-update) | async-done | bytes 1572880 | tf_op jit(solution)/shard_map/reduce_scatter | solution.py:254
  905.6 354.1 %reduce-scatter.9.cloned.1.call-done = f32[128,5248]{1,0:T(8,128)} async-done(((f32[1024,5248]{1,0:T(8,128)}), f32[128,5248]{1,0:T(8,128)}) %reduce-scatter.9.cloned.1.call-update) | async-done | bytes 2686992 | tf_op jit(solution)/shard_map/reduce_scatter | solution.py:256
  1261.5 5.4 fusion.54
  1269.3 19.9 %all-reduce.2 = (f32[1024]{0:T(1024)S(1)}, f32[1024]{0:T(1024)S(1)}) all-reduce(f32[1024]{0:T(1024)S(1)} %get-tuple-element.166, f32[1024]{0:T(1024)S(1)} %get-tuple-element.164), channel_id=7, replica_groups=mesh['rep'=4,'fsdp'=2,'cp'=4] {'fsdp','cp'}, use_global_device_ids=true, to_apply=%region_25.26.clone | all-reduce | flops 2048 | bytes 16384
  1289.3 7.0 all-reduce.3
  1297.3 81.2 %all-reduce.7.cloned.1.call-done = (f32[128,3072]{1,0:T(8,128)}, f32[128,1024]{1,0:T(8,128)}, f32[128,5248]{1,0:T(8,128)}, f32[2624,128]{1,0:T(8,128)}) async-done(((f32[128,3072]{1,0:T(8,128)}, f32[128,1024]{1,0:T(8,128)}, f32[128,5248]{1,0:T(8,128)}, f32[2624,128]{1,0:T(8,128)}), (f32[128,3072]{1,0:T(8,128)}, f32[128,1024]{1,0:T(8,128)}, f32[128,5248]{1,0:T(8,128)}, ...) | async-done | bytes 6127632 | tf_op jit(solution)/shard_map/psum | solution.py:261
  1378.4 2.9 copy.67
  (180 shorter events, 65.3 us)
Async XLA Ops:
  7.2 2.9 copy-start.14
  7.2 25.6 %copy-start.13 = (s32[1,128]{1,0:T(1,128)S(1)}, s32[1,128]{1,0:T(1,128)}, u32[]{:S(2)}) copy-start(s32[1,128]{1,0:T(1,128)} %param.14) | copy-start | bytes 1540
  7.2 33.5 %copy-start.15 = (bf16[128]{0:T(256)(128)(2,1)S(1)}, bf16[128]{0:T(256)(128)(2,1)}, u32[]{:S(2)}) copy-start(bf16[128]{0:T(256)(128)(2,1)} %param.21) | copy-start | bytes 772
  7.2 53.1 %copy-start = (bf16[1,128,1024]{2,1,0:T(8,128)(2,1)S(1)}, bf16[1,128,1024]{2,1,0:T(8,128)(2,1)}, u32[]{:S(2)}) copy-start(bf16[1,128,1024]{2,1,0:T(8,128)(2,1)} %param.13) | copy-start | bytes 786436
  7.2 104.5 %all-gather.8.cloned.1.call-start = ((), (), s32[]{:S(2)}) async-start(), calls=%async_computation.4 | async-start | bytes 7077888 | tf_op jit(solution)/shard_map/all_gather | solution.py:164
  7.9 155.8 %all-gather.10.cloned.1.call-start = ((), (), s32[]{:S(2)}) async-start(), calls=%async_computation.5 | async-start | bytes 2359296 | tf_op jit(solution)/shard_map/all_gather | solution.py:165
  8.7 309.4 %all-gather.12.cloned.1.call-start = ((), (), s32[]{:S(2)}) async-start(), calls=%async_computation.6 | async-start | bytes 12091392 | tf_op jit(solution)/shard_map/all_gather | solution.py:166
  9.4 397.1 %all-gather.14.cloned.1.call-start = ((), (), s32[]{:S(2)}) async-start(), calls=%async_computation.7 | async-start | bytes 6045696 | tf_op jit(solution)/shard_map/all_gather | solution.py:167
  10.0 499.9 %reduce-scatter.7.cloned.1.call-start = ((), (), s32[]{:S(2)}) async-start(), calls=%async_computation.9 | async-start | bytes 4718592 | tf_op jit(solution)/shard_map/reduce_scatter | solution.py:255
  125.1 13.7 collective-permute-start.1
  126.4 12.4 collective-permute-start
  131.2 14.6 %collective-permute-start.3 = (bf16[128,1024]{0,1:T(8,128)(2,1)S(1)}, bf16[128,1024]{0,1:T(8,128)(2,1)S(1)}, u32[]{:S(2)}, u32[]{:S(2)}) collective-permute-start(bf16[128,1024]{0,1:T(8,128)(2,1)S(1)} %bitcast.278), channel_id=1, source_target_pairs={{1,0},{2,1},{3,2},{5,4},{6,5},{7,6},{9,8},{10,9},{11,10},{13,12},{... | collective-permute-start | bytes 786440 | tf_op jit(solution)/shard_map/ppermute | solution.py:20
  132.5 13.3 collective-permute-start.2
  150.9 12.8 copy-start.3
  318.1 88.5 %copy-start.7 = (bf16[1,128,1024]{2,1,0:T(8,128)(2,1)S(1)}, bf16[1,128,1024]{2,1,0:T(8,128)(2,1)}, u32[]{:S(2)}) copy-start(bf16[1,128,1024]{2,1,0:T(8,128)(2,1)} %param.15) | copy-start | bytes 786436
  411.9 8.3 copy-start.8
  411.9 8.3 copy-start.10
  423.2 272.2 %reduce-scatter.11.cloned.1.call-start = ((), (), s32[]{:S(2)}) async-start(), calls=%async_computation.11 | async-start | bytes 12091392 | tf_op jit(solution)/shard_map/reduce_scatter | solution.py:257
  431.0 474.6 %reduce-scatter.5.cloned.1.call-start = ((), (), s32[]{:S(2)}) async-start(), calls=%async_computation.8 | async-start | bytes 14155776 | tf_op jit(solution)/shard_map/reduce_scatter | solution.py:254
  457.1 4.7 copy-start.4
  458.9 10.7 collective-permute-start.5
  460.5 9.7 collective-permute-start.4
  462.1 8.2 copy-start.12
  462.1 11.3 collective-permute-start.7
  467.2 8.7 collective-permute-start.6
  483.4 776.2 %reduce-scatter.9.cloned.1.call-start = ((), (), s32[]{:S(2)}) async-start(), calls=%async_computation.10 | async-start | bytes 24182784 | tf_op jit(solution)/shard_map/reduce_scatter | solution.py:256
  493.9 884.6 %all-reduce.7.cloned.1.call-start = ((), (), s32[]{:S(2)}) async-start(), calls=%async_computation.12 | async-start | bytes 12255232 | tf_op jit(solution)/shard_map/psum | solution.py:261
  1259.6 7.3 slice-start
  1261.5 5.4 slice-start.1
  1261.5 5.4 copy-start.2
  1378.4 4.7 copy-start.5
  1383.2 2.3 copy-start.6
  (4 other events, 3.9 us)
Sparse Core Ops, SparseCore 0:
  10.1 101.5 all-gather.7
  113.8 49.8 all-gather.9
  165.8 152.2 all-gather.11
  320.0 86.5 all-gather.13
  423.3 86.6 reduce-scatter.6
  513.4 181.9 reduce-scatter.10
  699.0 206.5 reduce-scatter.4
  909.5 350.1 reduce-scatter.8
  1262.2 116.1 all-reduce.6
where the time goes:
time: 1390 us
  waiting for transfers between devices  1160 us (83%)
  matrix products  88.6 us (6%)
  blocking collectives  76.2 us (5%)
  local copies, waits for them, and re-layouts  23.6 us (2%)
  starting transfers between devices  21.5 us (2%)
  between operations  15 us (1%)
    reduce_scatter x1, waiting for transfers between devices, shards(): lax.psum_scatter(grad_in, ('fsdp', 'cp'), scatter_dimension=0, tiled=True)  354 us
    reduce_scatter x1, waiting for transfers between devices, shards(): lax.psum_scatter(grad_qkv, ('fsdp', 'cp'), scatter_dimension=0, tiled=True)  210 us
    reduce_scatter x1, waiting for transfers between devices, shards(): lax.psum_scatter(grad_mlp, ('fsdp', 'cp'), scatter_dimension=1, tiled=True)  185 us
    all_gather x1, waiting for transfers between devices, shards(): lax.all_gather(w_in, ('fsdp', 'cp'), axis=0, tiled=True)  152 us
    psum x1, waiting for transfers between devices, shards(): lax.psum((owned[0], owned[1], owned[2], owned[3], owned[4], owned[5]), 'r...  81.2 us
    all_gather x1, waiting for transfers between devices, shards(): lax.all_gather(w_mlp, ('fsdp', 'cp'), axis=1, tiled=True)  81.2 us
    all_gather x1, waiting for transfers between devices, shards(): lax.all_gather(w_qkv, ('fsdp', 'cp'), axis=0, tiled=True)  50.7 us
  transfers between devices with their start and end apart: 17, of which 14 were waited for; matrix products, arithmetic and copies ran while one was open for 7% of the time, Pallas kernels for 0%

commit v1 on v0

--- a/solution.py
+++ b/solution.py
@@ -119,36 +119,101 @@
 
 
 def fetch_near(keys_local, values_local, reach):
-    key_parts = []
-    value_parts = []
+    width = keys_local.shape[1]
+    both = jnp.concatenate([keys_local, values_local], 1)
+    parts = []
     for offset in range(-reach, reach + 1):
-        if offset == 0:
-            key_parts.append(keys_local)
-            value_parts.append(values_local)
-        else:
-            got_k, got_v = from_behind((keys_local, values_local), "cp", -offset)
-            key_parts.append(got_k)
-            value_parts.append(got_v)
-    return (jnp.concatenate(key_parts, 0), jnp.concatenate(value_parts, 0))
+        parts.append(both if offset == 0 else from_behind(both, "cp", -offset))
+    joined = jnp.concatenate(parts, 0)
+    return (joined[:, :width], joined[:, width:])
 
 
 def return_near(grad_keys, grad_values, reach, rows):
+    width = grad_keys.shape[1]
     own_k = grad_keys[reach * rows : (reach + 1) * rows]
     own_v = grad_values[reach * rows : (reach + 1) * rows]
+    both = jnp.concatenate([grad_keys, grad_values], 1).astype(jnp.bfloat16)
     for offset in range(-reach, reach + 1):
         if offset != 0:
             lower = (reach + offset) * rows
-            got_k, got_v = (
-                from_behind(
-                    grad_keys[lower : lower + rows].astype(jnp.bfloat16), "cp", offset
-                ).astype(jnp.float32),
-                from_behind(
-                    grad_values[lower : lower + rows].astype(jnp.bfloat16), "cp", offset
-                ).astype(jnp.float32),
-            )
-            own_k = own_k + got_k
-            own_v = own_v + got_v
+            got = from_behind(both[lower : lower + rows], "cp", offset).astype(jnp.float32)
+            own_k = own_k + got[:, :width]
+            own_v = own_v + got[:, width:]
     return (own_k, own_v)
+
+
+def swap(value, axis, mask):
+    return lax.ppermute(value, axis, [(i, i ^ mask) for i in range(lax.axis_size(axis))])
+
+
+def side(axis, mask):
+    return (lax.axis_index(axis) // mask) % 2
+
+
+def masks(axis):
+    found = []
+    mask = lax.axis_size(axis) // 2
+    while mask:
+        found.append((axis, mask))
+        mask //= 2
+    return found
+
+
+def digits():
+    return masks("fsdp") + masks("cp") + masks("rep")
+
+
+def order(turn):
+    rep = masks("rep")
+    rest = [rep[:-1], masks("fsdp"), masks("cp")[::-1]]
+    steps = rep[-1:]
+    for i in range(3):
+        steps = steps + rest[(turn + i) % 3]
+    return steps
+
+
+def reduce_rows(value, turn):
+    left = digits()
+    rows, columns = value.shape
+    value = value.reshape([2] * len(left) + [rows // 2 ** len(left), columns])
+    for axis, mask in order(turn):
+        dim = left.index((axis, mask))
+        left.remove((axis, mask))
+        mine = side(axis, mask)
+        keep = lax.dynamic_index_in_dim(value, mine, dim, False).astype(jnp.float32)
+        send = lax.dynamic_index_in_dim(value, 1 - mine, dim, False).astype(jnp.bfloat16)
+        value = keep + swap(send, axis, mask).astype(jnp.float32)
+        if left:
+            value = value.astype(jnp.bfloat16)
+    for axis, mask in masks("rep"):
+        value = value.astype(jnp.bfloat16)
+        value = double(value[None] if value.ndim == 2 else value, axis, mask)
+    if masks("rep"):
+        count = len(masks("rep"))
+        value = value.reshape([2] * count + list(value.shape[-2:]))
+        value = value.transpose(list(range(count))[::-1] + [count, count + 1])
+    return value.reshape(-1, columns).astype(jnp.float32)
+
+
+def double(value, axis, mask):
+    mine = side(axis, mask)
+    got = swap(value, axis, mask)
+    return jnp.stack([jnp.where(mine == 0, value, got), jnp.where(mine == 0, got, value)])
+
+
+def gather_rows(local, turn):
+    copies = lax.axis_size("rep")
+    rows, columns = local.shape
+    part = rows // copies
+    value = lax.dynamic_slice_in_dim(local, lax.axis_index("rep") * part, part, 0)
+    steps = order(turn)[::-1]
+    for axis, mask in steps:
+        value = double(value, axis, mask)
+    outer = steps[::-1]
+    count = len(outer)
+    value = value.reshape([2] * count + [part, columns])
+    where = [outer.index(digit) for digit in digits()]
+    return value.transpose(where + [count, count + 1]).reshape(-1, columns)
 
 
 def shards(tokens, segments, cotangent, w_qkv, w_attn, w_in, w_mlp, gain_attn, gain_mlp):
@@ -160,16 +225,22 @@
     size = width // heads
     blocks = lax.axis_size("cp")
     position = lax.axis_index("cp")
-    full = (
-        lax.all_gather(w_qkv, ("fsdp", "cp"), axis=0, tiled=True),
-        lax.all_gather(w_attn, ("fsdp", "cp"), axis=0, tiled=True),
-        lax.all_gather(w_in, ("fsdp", "cp"), axis=0, tiled=True),
-        lax.all_gather(w_mlp, ("fsdp", "cp"), axis=1, tiled=True),
-        lax.all_gather(gain_attn, ("fsdp", "cp"), axis=0, tiled=True),
-        lax.all_gather(gain_mlp, ("fsdp", "cp"), axis=0, tiled=True),
-    )
-    f_qkv, f_attn, f_in, f_mlp, f_gone, f_gtwo = full
-    hidden = f_mlp.shape[0]
+    hidden = w_mlp.shape[0]
+    gains = jnp.stack([gain_attn, gain_mlp], 1)
+    gains = jnp.pad(gains, ((0, 0), (0, 126)))
+    wq = gather_rows(jnp.concatenate([w_qkv[:, :width], gains], 1), 0)
+    wk = gather_rows(w_qkv[:, width : 2 * width], 1)
+    wv = gather_rows(w_qkv[:, 2 * width :], 2)
+    wq, wk, wv, late_attn, late_in, late_mlp = lax.optimization_barrier(
+        (wq, wk, wv, w_attn, w_in, w_mlp)
+    )
+    f_gains = wq[:, width : width + 2].T
+    f_gone, f_gtwo = f_gains[0], f_gains[1]
+    wq = wq[:, :width]
+    f_attn = gather_rows(late_attn, 1)
+    wa = gather_rows(late_in[:, :hidden], 0)
+    wg = gather_rows(late_in[:, hidden:], 1)
+    wm = gather_rows(late_mlp.T, 2)
     key_segments = lax.all_gather(local_segments, "cp", axis=0, tiled=True)
     index = position * rows + jnp.arange(rows, dtype=jnp.int32)
     start = jnp.sum((key_segments[None, :] < local_segments[:, None]).astype(jnp.int32), 1)
@@ -181,10 +252,11 @@
     inputs = local_tokens.astype(jnp.float32)
     n_one, r_one = layer_norm(inputs)
     h_one = (n_one * g_one).astype(jnp.bfloat16)
-    qkv = jnp.dot(h_one, f_qkv, preferred_element_type=jnp.float32).reshape(rows, 3, heads, size)
-    query = rotate(qkv[:, 0], cosine, sine).astype(jnp.bfloat16)
-    keys_local = rotate(qkv[:, 1], cosine, sine).astype(jnp.bfloat16).reshape(rows, width)
-    values_local = qkv[:, 2].astype(jnp.bfloat16).reshape(rows, width)
+    key_raw = jnp.dot(h_one, wk, preferred_element_type=jnp.float32).reshape(rows, heads, size)
+    keys_local = rotate(key_raw, cosine, sine).astype(jnp.bfloat16).reshape(rows, width)
+    values_local = jnp.dot(h_one, wv, preferred_element_type=jnp.float32).astype(jnp.bfloat16)
+    query_raw = jnp.dot(h_one, wq, preferred_element_type=jnp.float32).reshape(rows, heads, size)
+    query = rotate(query_raw, cosine, sine).astype(jnp.bfloat16)
     offsets = jnp.arange(-reach, reach + 1, dtype=jnp.int32)
     block_ids = position + offsets
     inside = (block_ids >= 0) & (block_ids < blocks)
@@ -202,37 +274,32 @@
     x_two = inputs + jnp.dot(flat_mixed, f_attn, preferred_element_type=jnp.float32)
     n_two, r_two = layer_norm(x_two)
     h_two = (n_two * g_two).astype(jnp.bfloat16)
-    proj = jnp.dot(h_two, f_in, preferred_element_type=jnp.float32)
-    act_in, gate = (proj[:, :hidden], proj[:, hidden:])
+    act_in = jnp.dot(h_two, wa, preferred_element_type=jnp.float32)
+    gate = jnp.dot(h_two, wg, preferred_element_type=jnp.float32)
     act, slope = gelu_parts(act_in)
     inner = (act * gate).astype(jnp.bfloat16)
-    output = (x_two + jnp.dot(inner, f_mlp, preferred_element_type=jnp.float32)).astype(
+    output = (x_two + jnp.dot(inner, wm.T, preferred_element_type=jnp.float32)).astype(
         jnp.bfloat16
     )
-    back = (
-        lax.all_gather(w_qkv, ("fsdp", "cp"), axis=0, tiled=True),
-        lax.all_gather(w_attn, ("fsdp", "cp"), axis=0, tiled=True),
-        lax.all_gather(w_in, ("fsdp", "cp"), axis=0, tiled=True),
-        lax.all_gather(w_mlp, ("fsdp", "cp"), axis=1, tiled=True),
-        lax.all_gather(gain_attn, ("fsdp", "cp"), axis=0, tiled=True),
-        lax.all_gather(gain_mlp, ("fsdp", "cp"), axis=0, tiled=True),
-    )
-    b_qkv, b_attn, b_in, b_mlp, b_gone, b_gtwo = back
-    bg_one = b_gone.astype(jnp.float32)
-    bg_two = b_gtwo.astype(jnp.float32)
     grad_out = local_cotangent.astype(jnp.float32)
-    grad_mlp = jnp.dot(inner.T, local_cotangent, preferred_element_type=jnp.float32)
-    grad_inner = jnp.dot(local_cotangent, b_mlp.T, preferred_element_type=jnp.float32)
-    grad_proj = jnp.concatenate([grad_inner * gate * slope, grad_inner * act], -1).astype(
-        jnp.bfloat16
-    )
-    grad_in = jnp.dot(h_two.T, grad_proj, preferred_element_type=jnp.float32)
-    grad_h_two = jnp.dot(grad_proj, b_in.T, preferred_element_type=jnp.float32)
+    grad_mlp = jnp.dot(local_cotangent.T, inner, preferred_element_type=jnp.float32)
+    sum_mlp = reduce_rows(grad_mlp.astype(jnp.bfloat16), 2)
+    grad_inner = jnp.dot(local_cotangent, wm, preferred_element_type=jnp.float32)
+    grad_act = (grad_inner * gate * slope).astype(jnp.bfloat16)
+    grad_gate = (grad_inner * act).astype(jnp.bfloat16)
+    grad_ina = jnp.dot(h_two.T, grad_act, preferred_element_type=jnp.float32)
+    grad_ing = jnp.dot(h_two.T, grad_gate, preferred_element_type=jnp.float32)
+    sum_ina = reduce_rows(grad_ina.astype(jnp.bfloat16), 0)
+    sum_ing = reduce_rows(grad_ing.astype(jnp.bfloat16), 1)
+    grad_h_two = jnp.dot(grad_act, wa.T, preferred_element_type=jnp.float32) + jnp.dot(
+        grad_gate, wg.T, preferred_element_type=jnp.float32
+    )
     grad_g_two = jnp.sum(grad_h_two * n_two, 0)
-    grad_x_two = grad_out + norm_back(grad_h_two * bg_two, n_two, r_two)
+    grad_x_two = grad_out + norm_back(grad_h_two * g_two, n_two, r_two)
     grad_a = grad_x_two.astype(jnp.bfloat16)
     grad_attn = jnp.dot(flat_mixed.T, grad_a, preferred_element_type=jnp.float32)
-    grad_mixed = jnp.dot(grad_a, b_attn.T, preferred_element_type=jnp.float32).astype(jnp.bfloat16)
+    sum_attn = reduce_rows(grad_attn.astype(jnp.bfloat16), 1)
+    grad_mixed = jnp.dot(grad_a, f_attn.T, preferred_element_type=jnp.float32).astype(jnp.bfloat16)
     back_keys, back_values = (keys, values)
     grad_q, grad_k_all, grad_v_all = attend_back(
         query, back_keys, back_values, mixed_b, grad_mixed.reshape(rows, heads, size), lse, same
@@ -242,32 +309,33 @@
     )
     grad_q = unrotate(grad_q, cosine, sine)
     grad_k = unrotate(grad_k_own.reshape(rows, heads, size), cosine, sine)
-    grad_v = grad_v_own.reshape(rows, heads, size)
-    grad_qkv_rows = (
-        jnp.stack([grad_q, grad_k, grad_v], 1).reshape(rows, 3 * width).astype(jnp.bfloat16)
-    )
-    grad_qkv = jnp.dot(h_one.T, grad_qkv_rows, preferred_element_type=jnp.float32)
-    grad_h_one = jnp.dot(grad_qkv_rows, b_qkv.T, preferred_element_type=jnp.float32)
+    row_q = grad_q.reshape(rows, width).astype(jnp.bfloat16)
+    row_k = grad_k.reshape(rows, width).astype(jnp.bfloat16)
+    row_v = grad_v_own.astype(jnp.bfloat16)
+    h_t = h_one.T
+    grad_wq = jnp.dot(h_t, row_q, preferred_element_type=jnp.float32).astype(jnp.bfloat16)
+    grad_wk = jnp.dot(h_t, row_k, preferred_element_type=jnp.float32).astype(jnp.bfloat16)
+    grad_wv = jnp.dot(h_t, row_v, preferred_element_type=jnp.float32).astype(jnp.bfloat16)
+    grad_h_one = (
+        jnp.dot(row_q, wq.T, preferred_element_type=jnp.float32)
+        + jnp.dot(row_k, wk.T, preferred_element_type=jnp.float32)
+        + jnp.dot(row_v, wv.T, preferred_element_type=jnp.float32)
+    )
     grad_g_one = jnp.sum(grad_h_one * n_one, 0)
-    grad_tokens = (grad_x_two + norm_back(grad_h_one * bg_one, n_one, r_one)).astype(jnp.bfloat16)
-    owned = (
-        lax.psum_scatter(grad_qkv, ("fsdp", "cp"), scatter_dimension=0, tiled=True),
-        lax.psum_scatter(grad_attn, ("fsdp", "cp"), scatter_dimension=0, tiled=True),
-        lax.psum_scatter(grad_in, ("fsdp", "cp"), scatter_dimension=0, tiled=True),
-        lax.psum_scatter(grad_mlp, ("fsdp", "cp"), scatter_dimension=1, tiled=True),
-        lax.psum_scatter(grad_g_one, ("fsdp", "cp"), scatter_dimension=0, tiled=True),
-        lax.psum_scatter(grad_g_two, ("fsdp", "cp"), scatter_dimension=0, tiled=True),
-    )
-    summed = lax.psum((owned[0], owned[1], owned[2], owned[3], owned[4], owned[5]), "rep")
+    grad_tokens = (grad_x_two + norm_back(grad_h_one * g_one, n_one, r_one)).astype(jnp.bfloat16)
+    grad_gains = jnp.pad(jnp.stack([grad_g_one, grad_g_two], 1), ((0, 0), (0, 126)))
+    sum_q = reduce_rows(jnp.concatenate([grad_wq, grad_gains.astype(jnp.bfloat16)], 1), 0)
+    sum_k = reduce_rows(grad_wk, 1)
+    sum_v = reduce_rows(grad_wv, 2)
     return (
         output[None],
         grad_tokens[None],
-        summed[0],
-        summed[1],
-        summed[2],
-        summed[3],
-        summed[4],
-        summed[5],
+        jnp.concatenate([sum_q[:, :width], sum_k, sum_v], 1),
+        sum_attn,
+        jnp.concatenate([sum_ina, sum_ing], 1),
+        sum_mlp.T,
+        sum_q[:, width],
+        sum_q[:, width + 1],
     )
 
 

time: 1390 us -> 600 us (0.43); the launches traced: 1390 us -> 589 us
  waiting for transfers between devices: 1160 us -> 244 us
  starting transfers between devices: 21.5 us -> 103 us
  blocking collectives: 76.2 us -> 9.14 us
  other arithmetic: 7.24 us -> 73.4 us
  local copies, waits for them, and re-layouts: 23.6 us -> 87 us
  matrix products: 88.6 us -> 68.8 us
    reduce_scatter x4 -> x0, waiting for transfers between devices: 766 us -> none  [the longest x1 354 us: shards(): lax.psum_scatter(grad_in, ('fsdp', 'cp'), scatter_dimension=0, tiled=True)]
    all_gather x4 -> x0, waiting for transfers between devices: 297 us -> none  [the longest x1 152 us: shards(): lax.all_gather(w_in, ('fsdp', 'cp'), axis=0, tiled=True)]
    ppermute x0 -> x84, waiting for transfers between devices: none -> 244 us  [swap(): lax.ppermute(value, axis, [(i, i ^ mask) for i in range(lax.axis_size(axi...]
    ppermute x0 -> x84, starting transfers between devices: none -> 90.4 us  [swap(): lax.ppermute(value, axis, [(i, i ^ mask) for i in range(lax.axis_size(axi...]
    psum x1 -> x0, waiting for transfers between devices: 81.2 us -> none  [shards(): lax.psum((owned[0], owned[1], owned[2], owned[3], owned[4], owned[5]), 'r...]
    all_gather x2 -> x0, blocking collectives: 41.4 us -> none  [the longest x1 22.7 us: shards(): lax.all_gather(gain_attn, ('fsdp', 'cp'), axis=0, tiled=True)]
    another operation x8 -> x99, other arithmetic: 1.9 us -> 37.6 us  [the longest x91 35 us: double(): jnp.stack([jnp.where(mine == 0, value, got), jnp.where(mine == 0, got, va...]
    convert_element_type x1 -> x11, local copies, waits for them, and re-layouts: 1.12 us -> 26.3 us  [the longest x1 8.34 us: shards(): sum_mlp = reduce_rows(grad_mlp.astype(jnp.bfloat16), 2)]
  transfers between devices with their start and end apart: 17 -> 88, of which waited for: 14 -> 43; matrix products, arithmetic and copies ran while one was open for 7% -> 23% of each run, Pallas kernels for 0% -> 0%
where the time goes in v1:
time: 600 us; the launch traced here: 589 us
  waiting for transfers between devices  244 us (41%)
  starting transfers between devices  103 us (17%)
  local copies, waits for them, and re-layouts  87 us (14%)
  other arithmetic  73.4 us (12%)
  matrix products  68.8 us (11%)
  blocking collectives  9.14 us (2%)
    ppermute x84, waiting for transfers between devices, swap(): lax.ppermute(value, axis, [(i, i ^ mask) for i in range(lax.axis_size(axi...  244 us
    ppermute x84, starting transfers between devices, swap(): lax.ppermute(value, axis, [(i, i ^ mask) for i in range(lax.axis_size(axi...  90.4 us
    another operation x91, other arithmetic, double(): jnp.stack([jnp.where(mine == 0, value, got), jnp.where(mine == 0, got, va...  35 us
    convert_element_type x28, other arithmetic, reduce_rows(): value = value.astype(jnp.bfloat16)  15 us
    ppermute x4, starting transfers between devices, from_behind(): lax.ppermute(value, axis, [(source, source + steps) for source in range(i...  12.3 us
  transfers between devices with their start and end apart: 88, of which 43 were waited for; matrix products, arithmetic and copies ran while one was open for 23% of the time, Pallas kernels for 0%

profile of v1, /device:TPU:0, one launch (start us, length us, event | category | flops | bytes accessed | tf_op | source)
XLA Modules:
  0.0 589.0 jit_solution(6663365661725021301)
XLA Ops:
  2.7 4.1 collective-permute-start
  10.3 9.1 %all-gather = s32[1,512]{1,0:T(1,128)S(1)} all-gather(s32[1,128]{1,0:T(1,128)S(1)} %copy-done.53), channel_id=2, replica_groups=mesh['rep'=4,'fsdp'=2,'cp'=4] {'cp'}, dimensions={1}, use_global_device_ids=true | all-gather | bytes 2560 | tf_op jit(solution)/shard_map/all_gather | solution.py:244
  22.3 5.9 collective-permute-done.6
  32.0 6.2 %collective-permute-done.7 = bf16[2,2,32,1024]{3,2,1,0:T(8,128)(2,1)S(1)} collective-permute-done((bf16[2,2,32,1024]{3,2,1,0:T(8,128)(2,1)S(1)}, bf16[2,2,32,1024]{3,2,1,0:T(8,128)(2,1)S(1)}, u32[]{:S(2)}, u32[]{:S(2)}) %collective-permute-start.7) | collective-permute-done | bytes 262176 | tf_op jit(solution)/shard_map/ppermute | solution.py:146
  41.8 9.2 %collective-permute-done.8 = bf16[2,2,2,32,1024]{4,3,2,0,1:T(8,128)(2,1)S(1)} collective-permute-done((bf16[2,2,2,32,1024]{4,3,2,0,1:T(8,128)(2,1)S(1)}, bf16[2,2,2,32,1024]{4,3,2,0,1:T(8,128)(2,1)S(1)}, u32[]{:S(2)}, u32[]{:S(2)}) %collective-permute-start.8) | collective-permute-done | bytes 524320 | tf_op jit(solution)/shard_map/ppermute | solution.py:146
  82.9 5.4 collective-permute-start.15
  100.4 7.1 %collective-permute-done.22 = bf16[32,2624]{1,0:T(8,128)(2,1)S(1)} collective-permute-done((bf16[32,2624]{1,0:T(8,128)(2,1)S(1)}, bf16[32,2624]{1,0:T(8,128)(2,1)S(1)}, u32[]{:S(2)}, u32[]{:S(2)}) %collective-permute-start.22) | collective-permute-done | bytes 167968 | tf_op jit(solution)/shard_map/ppermute | solution.py:146
  110.2 10.9 %collective-permute-start.19 = (bf16[2,2,32,1024]{3,2,1,0:T(8,128)(2,1)S(1)}, bf16[2,2,32,1024]{3,2,1,0:T(8,128)(2,1)S(1)}, u32[]{:S(2)}, u32[]{:S(2)}) collective-permute-start(bf16[2,2,32,1024]{3,2,1,0:T(8,128)(2,1)S(1)} %pad_maximum_fusion.35), channel_id=1, source_target_pairs={{0,1},{1,0},{2,3},{3,2},{4,5},{5,4},{6,7},{7,6},{8,9},{9,8},{10,11... | collective-permute-start | bytes 786440 | tf_op jit(solution)/shard_map/ppermute | solution.py:146
  121.2 6.3 %collective-permute-done.19 = bf16[2,2,32,1024]{3,2,1,0:T(8,128)(2,1)S(1)} collective-permute-done((bf16[2,2,32,1024]{3,2,1,0:T(8,128)(2,1)S(1)}, bf16[2,2,32,1024]{3,2,1,0:T(8,128)(2,1)S(1)}, u32[]{:S(2)}, u32[]{:S(2)}) %collective-permute-start.19) | collective-permute-done | bytes 262176 | tf_op jit(solution)/shard_map/ppermute | solution.py:146
  130.9 8.3 %collective-permute-start.34 = (bf16[2,2,32,2624]{3,2,1,0:T(8,128)(2,1)}, bf16[2,2,32,2624]{3,2,1,0:T(8,128)(2,1)}, u32[]{:S(2)}, u32[]{:S(2)}) collective-permute-start(bf16[2,2,32,2624]{3,2,1,0:T(8,128)(2,1)} %pad_maximum_fusion.17), channel_id=1, source_target_pairs={{0,2},{1,3},{2,0},{3,1},{4,6},{5,7},{6,4},{7,5},{8,10},{9,11},{10,... | collective-permute-start | bytes 2015240 | tf_op jit(solution)/shard_map/ppermute | solution.py:146
  144.8 5.2 while.30
  152.6 16.8 %collective-permute-done.34 = bf16[2,2,32,2624]{3,2,1,0:T(8,128)(2,1)} collective-permute-done((bf16[2,2,32,2624]{3,2,1,0:T(8,128)(2,1)}, bf16[2,2,32,2624]{3,2,1,0:T(8,128)(2,1)}, u32[]{:S(2)}, u32[]{:S(2)}) %collective-permute-start.34) | collective-permute-done | bytes 671776 | tf_op jit(solution)/shard_map/ppermute | solution.py:146
  177.5 24.4 %collective-permute-done.35 = bf16[2,2,2,32,2624]{4,3,2,1,0:T(8,128)(2,1)S(1)} collective-permute-done((bf16[2,2,2,32,2624]{4,3,2,1,0:T(8,128)(2,1)S(1)}, bf16[2,2,2,32,2624]{4,3,2,1,0:T(8,128)(2,1)S(1)}, u32[]{:S(2)}, u32[]{:S(2)}) %collective-permute-start.35) | collective-permute-done | bytes 1343520 | tf_op jit(solution)/shard_map/ppermute | solution.py:146
  251.0 25.5 %while.31 = (s32[]{:T(128)}, f32[4,128,4,64]{1,3,2,0:T(8,128)}, f32[4,384,4,64]{1,3,2,0:T(8,128)}, f32[4,384,4,64]{1,3,2,0:T(8,128)}, bf16[4,384,4,64]{1,3,2,0:T...) while((s32[]{:T(128)}, f32[4,128,4,64]{1,3,2,0:T(8,128)}, ...), condition=%wide.region_13.14_spmd.clone.clone, body=%wide.region_11.13_spmd.clone.sunk.clone | while | flops 127565312 | bytes 5555725 | solution.py:117
  279.6 4.4 collective-permute-start.38
  290.2 7.8 %copy.298 = bf16[1024,2624]{1,0:T(8,128)(2,1)} copy(bf16[1024,2624]{0,1:T(8,128)(2,1)} %convolution_convert_fusion) | data formatting | bytes 10747904 | tf_op jit(solution)/shard_map/convert_element_type | solution.py:293
  298.0 4.6 constant_dynamic-slice_fusion.4
  304.8 7.8 %copy.292 = bf16[1024,2624]{1,0:T(8,128)(2,1)} copy(bf16[1024,2624]{0,1:T(8,128)(2,1)} %convolution_convert_fusion.1) | data formatting | bytes 10747904 | tf_op jit(solution)/shard_map/convert_element_type | solution.py:292
  320.3 8.3 %copy.306 = bf16[1024,2624]{1,0:T(8,128)(2,1)} copy(bf16[1024,2624]{0,1:T(8,128)(2,1)} %fusion.50) | data formatting | bytes 10747904 | tf_op jit(solution)/shard_map/convert_element_type | solution.py:286
  328.7 4.7 constant_dynamic-slice_fusion.2
  361.2 9.4 %collective-permute-done.61 = bf16[2,2,2,32,1024]{4,3,2,0,1:T(8,128)(2,1)} collective-permute-done((bf16[2,2,2,32,1024]{4,3,2,0,1:T(8,128)(2,1)}, bf16[2,2,2,32,1024]{4,3,2,0,1:T(8,128)(2,1)}, u32[]{:S(2)}, u32[]{:S(2)}) %collective-permute-start.61) | collective-permute-done | bytes 524320 | tf_op jit(solution)/shard_map/ppermute | solution.py:146
  378.5 4.9 collective-permute-done.62
  383.5 4.7 collective-permute-start.63
  388.3 5.9 %collective-permute-done.63 = bf16[2,32,1024]{2,1,0:T(8,128)(2,1)S(1)} collective-permute-done((bf16[2,32,1024]{2,1,0:T(8,128)(2,1)S(1)}, bf16[2,32,1024]{2,1,0:T(8,128)(2,1)S(1)}, u32[]{:S(2)}, u32[]{:S(2)}) %collective-permute-start.63) | collective-permute-done | bytes 131104 | tf_op jit(solution)/shard_map/ppermute | solution.py:146
  408.5 7.0 %collective-permute-done.47 = bf16[2,2,2,32,1024]{4,3,2,1,0:T(8,128)(2,1)S(1)} collective-permute-done((bf16[2,2,2,32,1024]{4,3,2,1,0:T(8,128)(2,1)S(1)}, bf16[2,2,2,32,1024]{4,3,2,1,0:T(8,128)(2,1)S(1)}, u32[]{:S(2)}, u32[]{:S(2)}) %collective-permute-start.47) | collective-permute-done | bytes 524320 | tf_op jit(solution)/shard_map/ppermute | solution.py:146
  423.4 8.6 %collective-permute-done.55 = bf16[2,2,32,1024]{3,2,0,1:T(8,128)(2,1)S(1)} collective-permute-done((bf16[2,2,32,1024]{3,2,0,1:T(8,128)(2,1)S(1)}, bf16[2,2,32,1024]{3,2,0,1:T(8,128)(2,1)S(1)}, u32[]{:S(2)}, u32[]{:S(2)}) %collective-permute-start.55) | collective-permute-done | bytes 262176 | tf_op jit(solution)/shard_map/ppermute | solution.py:146
  439.8 6.4 %collective-permute-done.49 = bf16[2,32,1024]{2,1,0:T(8,128)(2,1)S(1)} collective-permute-done((bf16[2,32,1024]{2,1,0:T(8,128)(2,1)S(1)}, bf16[2,32,1024]{2,1,0:T(8,128)(2,1)S(1)}, u32[]{:S(2)}, u32[]{:S(2)}) %collective-permute-start.49) | collective-permute-done | bytes 131104 | tf_op jit(solution)/shard_map/ppermute | solution.py:146
  473.0 29.4 %collective-permute-done.43 = bf16[32,1152]{1,0:T(8,128)(2,1)S(1)} collective-permute-done((bf16[32,1152]{1,0:T(8,128)(2,1)S(1)}, bf16[32,1152]{1,0:T(8,128)(2,1)S(1)}, u32[]{:S(2)}, u32[]{:S(2)}) %collective-permute-start.43) | collective-permute-done | bytes 73760 | tf_op jit(solution)/shard_map/ppermute | solution.py:146
  516.3 25.5 %collective-permute-done.76 = bf16[2,2,32,2624]{3,2,1,0:T(8,128)(2,1)S(1)} collective-permute-done((bf16[2,2,32,2624]{3,2,1,0:T(8,128)(2,1)S(1)}, bf16[2,2,32,2624]{3,2,1,0:T(8,128)(2,1)S(1)}, u32[]{:S(2)}, u32[]{:S(2)}) %collective-permute-start.76) | collective-permute-done | bytes 671776 | tf_op jit(solution)/shard_map/ppermute | solution.py:146
  544.8 12.3 %collective-permute-done.83 = bf16[2,2,32,2624]{3,2,0,1:T(8,128)(2,1)S(1)} collective-permute-done((bf16[2,2,32,2624]{3,2,0,1:T(8,128)(2,1)S(1)}, bf16[2,2,32,2624]{3,2,0,1:T(8,128)(2,1)S(1)}, u32[]{:S(2)}, u32[]{:S(2)}) %collective-permute-start.83) | collective-permute-done | bytes 671776 | tf_op jit(solution)/shard_map/ppermute | solution.py:146
  558.7 4.5 collective-permute-done.77
  575.9 4.9 collective-permute-done.72
  (607 shorter events, 310.1 us)
Async XLA Ops:
  2.7 18.5 %collective-permute-start = (bf16[32,1152]{1,0:T(8,128)(2,1)S(1)}, bf16[32,1152]{1,0:T(8,128)(2,1)S(1)}, u32[]{:S(2)}, u32[]{:S(2)}) collective-permute-start(bf16[32,1152]{1,0:T(8,128)(2,1)S(1)} %fusion.143), channel_id=1, source_target_pairs={{0,2},{1,3},{2,0},{3,1},{4,6},{5,7},{6,4},{7,5},{8,10},{9,11},{10,... | collective-permute-start | bytes 221192 | tf_op jit(solution)/shard_map/ppermute | solution.py:146
  81.6 60.0 %collective-permute-start.16 = (bf16[128,2048]{1,0:T(8,128)(2,1)}, bf16[128,2048]{1,0:T(8,128)(2,1)}, u32[]{:S(2)}, u32[]{:S(2)}) collective-permute-start(bf16[128,2048]{1,0:T(8,128)(2,1)} %pad_maximum_fusion.23), channel_id=1, source_target_pairs={{1,0},{2,1},{3,2},{5,4},{6,5},{7,6},{9,8},{10,9},{11,10},{13,12},{... | collective-permute-start | bytes 1572872 | tf_op jit(solution)/shard_map/ppermute | solution.py:20
  82.9 59.6 %collective-permute-start.15 = (bf16[128,2048]{1,0:T(8,128)(2,1)}, bf16[128,2048]{1,0:T(8,128)(2,1)}, u32[]{:S(2)}, u32[]{:S(2)}) collective-permute-start(bf16[128,2048]{1,0:T(8,128)(2,1)} %pad_maximum_fusion.23), channel_id=1, source_target_pairs={{0,1},{1,2},{2,3},{4,5},{5,6},{6,7},{8,9},{9,10},{10,11},{12,13},{... | collective-permute-start | bytes 1572872 | tf_op jit(solution)/shard_map/ppermute | solution.py:20
  99.4 29.1 %collective-permute-start.33 = (bf16[2,32,2624]{2,1,0:T(8,128)(2,1)S(1)}, bf16[2,32,2624]{2,1,0:T(8,128)(2,1)S(1)}, u32[]{:S(2)}, u32[]{:S(2)}) collective-permute-start(bf16[2,32,2624]{2,1,0:T(8,128)(2,1)S(1)} %pad_maximum_fusion.27), channel_id=1, source_target_pairs={{0,16},{8,24},{16,0},{24,8},{1,17},{9,25},{17,1},{25,9},{2,18},{10... | collective-permute-start | bytes 1007624 | tf_op jit(solution)/shard_map/ppermute | solution.py:146
  107.5 23.4 %collective-permute-start.28 = (bf16[2,32,2624]{2,1,0:T(8,128)(2,1)S(1)}, bf16[2,32,2624]{2,1,0:T(8,128)(2,1)S(1)}, u32[]{:S(2)}, u32[]{:S(2)}) collective-permute-start(bf16[2,32,2624]{2,1,0:T(8,128)(2,1)S(1)} %pad_maximum_fusion.26), channel_id=1, source_target_pairs={{0,2},{1,3},{2,0},{3,1},{4,6},{5,7},{6,4},{7,5},{8,10},{9,11},{10,... | collective-permute-start | bytes 1007624 | tf_op jit(solution)/shard_map/ppermute | solution.py:146
  128.5 22.2 %collective-permute-start.20 = (bf16[2,2,2,32,1024]{4,3,2,0,1:T(8,128)(2,1)}, bf16[2,2,2,32,1024]{4,3,2,0,1:T(8,128)(2,1)}, u32[]{:S(2)}, u32[]{:S(2)}) collective-permute-start(bf16[2,2,2,32,1024]{4,3,2,0,1:T(8,128)(2,1)} %pad_maximum_fusion.24), channel_id=1, source_target_pairs={{0,4},{4,0},{1,5},{5,1},{2,6},{6,2},{3,7},{7,3},{8,12},{12,8},{9,1... | collective-permute-start | bytes 1572872 | tf_op jit(solution)/shard_map/ppermute | solution.py:146
  130.9 38.4 %collective-permute-start.34 = (bf16[2,2,32,2624]{3,2,1,0:T(8,128)(2,1)}, bf16[2,2,32,2624]{3,2,1,0:T(8,128)(2,1)}, u32[]{:S(2)}, u32[]{:S(2)}) collective-permute-start(bf16[2,2,32,2624]{3,2,1,0:T(8,128)(2,1)} %pad_maximum_fusion.17), channel_id=1, source_target_pairs={{0,2},{1,3},{2,0},{3,1},{4,6},{5,7},{6,4},{7,5},{8,10},{9,11},{10,... | collective-permute-start | bytes 2015240 | tf_op jit(solution)/shard_map/ppermute | solution.py:146
  140.5 30.5 %collective-permute-start.29 = (bf16[2,2,32,2624]{3,2,1,0:T(8,128)(2,1)}, bf16[2,2,32,2624]{3,2,1,0:T(8,128)(2,1)}, u32[]{:S(2)}, u32[]{:S(2)}) collective-permute-start(bf16[2,2,32,2624]{3,2,1,0:T(8,128)(2,1)} %pad_maximum_fusion.16), channel_id=1, source_target_pairs={{0,1},{1,0},{2,3},{3,2},{4,5},{5,4},{6,7},{7,6},{8,9},{9,8},{10,11... | collective-permute-start | bytes 2015240 | tf_op jit(solution)/shard_map/ppermute | solution.py:146
  141.6 31.8 %collective-permute-start.24 = (bf16[2,2,32,2624]{3,2,1,0:T(8,128)(2,1)}, bf16[2,2,32,2624]{3,2,1,0:T(8,128)(2,1)}, u32[]{:S(2)}, u32[]{:S(2)}) collective-permute-start(bf16[2,2,32,2624]{3,2,1,0:T(8,128)(2,1)} %pad_maximum_fusion.15), channel_id=1, source_target_pairs={{0,4},{4,0},{1,5},{5,1},{2,6},{6,2},{3,7},{7,3},{8,12},{12,8},{9,1... | collective-permute-start | bytes 2015240 | tf_op jit(solution)/shard_map/ppermute | solution.py:146
  152.5 23.6 %collective-permute-start.21 = (bf16[2,2,2,2,32,1024]{5,4,3,1,2,0:T(8,128)(2,1)S(1)}, bf16[2,2,2,2,32,1024]{5,4,3,1,2,0:T(8,128)(2,1)S(1)}, u32[]{:S(2)}, u32[]{:S(2)}) collective-permute-start(bf16[2,2,2,2,32,1024]{5,4,3,1,2,0:T(8,128)(2,1)S(1)} %pad_maximum_fusion.14), channel_id=1, source_target_pairs={{0,8},{8,0},{16,24},{24,16},{1,9},{9,1},{17,25},{25,17},{2,10},{10... | collective-permute-start | bytes 3145736 | tf_op jit(solution)/shard_map/ppermute | solution.py:146
  170.8 31.0 %collective-permute-start.35 = (bf16[2,2,2,32,2624]{4,3,2,1,0:T(8,128)(2,1)S(1)}, bf16[2,2,2,32,2624]{4,3,2,1,0:T(8,128)(2,1)S(1)}, u32[]{:S(2)}, u32[]{:S(2)}) collective-permute-start(bf16[2,2,2,32,2624]{4,3,2,1,0:T(8,128)(2,1)S(1)} %pad_maximum_fusion.10), channel_id=1, source_target_pairs={{0,1},{1,0},{2,3},{3,2},{4,5},{5,4},{6,7},{7,6},{8,9},{9,8},{10,11... | collective-permute-start | bytes 4030472 | tf_op jit(solution)/shard_map/ppermute | solution.py:146
  172.4 31.0 %collective-permute-start.30 = (bf16[2,2,2,32,2624]{4,3,2,1,0:T(8,128)(2,1)S(1)}, bf16[2,2,2,32,2624]{4,3,2,1,0:T(8,128)(2,1)S(1)}, u32[]{:S(2)}, u32[]{:S(2)}) collective-permute-start(bf16[2,2,2,32,2624]{4,3,2,1,0:T(8,128)(2,1)S(1)} %pad_maximum_fusion.9), channel_id=1, source_target_pairs={{0,4},{4,0},{1,5},{5,1},{2,6},{6,2},{3,7},{7,3},{8,12},{12,8},{9,1... | collective-permute-start | bytes 4030472 | tf_op jit(solution)/shard_map/ppermute | solution.py:146
  174.9 31.0 %collective-permute-start.25 = (bf16[2,2,2,32,2624]{4,3,2,1,0:T(8,128)(2,1)S(1)}, bf16[2,2,2,32,2624]{4,3,2,1,0:T(8,128)(2,1)S(1)}, u32[]{:S(2)}, u32[]{:S(2)}) collective-permute-start(bf16[2,2,2,32,2624]{4,3,2,1,0:T(8,128)(2,1)S(1)} %pad_maximum_fusion.8), channel_id=1, source_target_pairs={{0,16},{8,24},{16,0},{24,8},{1,17},{9,25},{17,1},{25,9},{2,18},{10... | collective-permute-start | bytes 4030472 | tf_op jit(solution)/shard_map/ppermute | solution.py:146
  279.6 58.3 %collective-permute-start.38 = (bf16[128,2048]{0,1:T(8,128)(2,1)}, bf16[128,2048]{0,1:T(8,128)(2,1)}, u32[]{:S(2)}, u32[]{:S(2)}) collective-permute-start(bf16[128,2048]{0,1:T(8,128)(2,1)} %get-tuple-element.299), channel_id=1, source_target_pairs={{0,1},{1,2},{2,3},{4,5},{5,6},{6,7},{8,9},{9,10},{10,11},{12,13},{... | collective-permute-start | bytes 1572872 | tf_op jit(solution)/shard_map/ppermute | solution.py:20
  283.9 55.1 %collective-permute-start.37 = (bf16[128,2048]{0,1:T(8,128)(2,1)}, bf16[128,2048]{0,1:T(8,128)(2,1)}, u32[]{:S(2)}, u32[]{:S(2)}) collective-permute-start(bf16[128,2048]{0,1:T(8,128)(2,1)} %get-tuple-element.298), channel_id=1, source_target_pairs={{1,0},{2,1},{3,2},{5,4},{6,5},{7,6},{9,8},{10,9},{11,10},{13,12},{... | collective-permute-start | bytes 1572872 | tf_op jit(solution)/shard_map/ppermute | solution.py:20
  290.2 63.1 %collective-permute-start.60 = (bf16[2,2,2,2,32,1024]{5,4,3,1,2,0:T(8,128)(2,1)}, bf16[2,2,2,2,32,1024]{5,4,3,1,2,0:T(8,128)(2,1)}, u32[]{:S(2)}, u32[]{:S(2)}) collective-permute-start(bf16[2,2,2,2,32,1024]{5,4,3,1,2,0:T(8,128)(2,1)} %bitcast.762), channel_id=1, source_target_pairs={{0,8},{8,0},{16,24},{24,16},{1,9},{9,1},{17,25},{25,17},{2,10},{10... | collective-permute-start | bytes 3145736 | tf_op jit(solution)/shard_map/ppermute | solution.py:146
  304.3 156.7 %collective-permute-start.74 = (bf16[2,2,2,2,32,2624]{5,4,3,1,2,0:T(8,128)(2,1)}, bf16[2,2,2,2,32,2624]{5,4,3,1,2,0:T(8,128)(2,1)}, u32[]{:S(2)}, u32[]{:S(2)}) collective-permute-start(bf16[2,2,2,2,32,2624]{5,4,3,1,2,0:T(8,128)(2,1)} %bitcast.761), channel_id=1, source_target_pairs={{0,8},{8,0},{16,24},{24,16},{1,9},{9,1},{17,25},{25,17},{2,10},{10... | collective-permute-start | bytes 8060936 | tf_op jit(solution)/shard_map/ppermute | solution.py:146
  316.4 147.9 %collective-permute-start.67 = (bf16[2,2,2,2,32,2624]{5,4,3,2,1,0:T(8,128)(2,1)}, bf16[2,2,2,2,32,2624]{5,4,3,2,1,0:T(8,128)(2,1)}, u32[]{:S(2)}, u32[]{:S(2)}) collective-permute-start(bf16[2,2,2,2,32,2624]{5,4,3,2,1,0:T(8,128)(2,1)} %dynamic-slice_bitcast_fusion), channel_id=1, source_target_pairs={{0,8},{8,0},{16,24},{24,16},{1,9},{9,1},{17,25},{25,17},{2,10},{10... | collective-permute-start | bytes 8060936 | tf_op jit(solution)/shard_map/ppermute | solution.py:146
  349.2 22.7 %collective-permute-start.53 = (bf16[2,2,2,2,32,1024]{5,4,0,3,1,2:T(8,128)(2,1)}, bf16[2,2,2,2,32,1024]{5,4,0,3,1,2:T(8,128)(2,1)}, u32[]{:S(2)}, u32[]{:S(2)}) collective-permute-start(bf16[2,2,2,2,32,1024]{5,4,0,3,1,2:T(8,128)(2,1)} %bitcast.763), channel_id=1, source_target_pairs={{0,8},{8,0},{16,24},{24,16},{1,9},{9,1},{17,25},{25,17},{2,10},{10... | collective-permute-start | bytes 3145736 | tf_op jit(solution)/shard_map/ppermute | solution.py:146
  350.8 23.3 %collective-permute-start.46 = (bf16[2,2,2,2,32,1024]{5,4,3,2,1,0:T(8,128)(2,1)}, bf16[2,2,2,2,32,1024]{5,4,3,2,1,0:T(8,128)(2,1)}, u32[]{:S(2)}, u32[]{:S(2)}) collective-permute-start(bf16[2,2,2,2,32,1024]{5,4,3,2,1,0:T(8,128)(2,1)} %dynamic-slice_bitcast_fusion.5), channel_id=1, source_target_pairs={{0,8},{8,0},{16,24},{24,16},{1,9},{9,1},{17,25},{25,17},{2,10},{10... | collective-permute-start | bytes 3145736 | tf_op jit(solution)/shard_map/ppermute | solution.py:146
  370.6 97.5 %collective-permute-start.81 = (bf16[2,2,2,2,32,2624]{5,4,0,3,1,2:T(8,128)(2,1)}, bf16[2,2,2,2,32,2624]{5,4,0,3,1,2:T(8,128)(2,1)S(1)}, u32[]{:S(2)}, u32[]{:S(2)}) collective-permute-start(bf16[2,2,2,2,32,2624]{5,4,0,3,1,2:T(8,128)(2,1)} %bitcast.868), channel_id=1, source_target_pairs={{0,8},{8,0},{16,24},{24,16},{1,9},{9,1},{17,25},{25,17},{2,10},{10... | collective-permute-start | bytes 8060936 | tf_op jit(solution)/shard_map/ppermute | solution.py:146
  371.9 23.1 %collective-permute-start.39 = (bf16[2,2,2,2,32,1152]{5,4,3,2,1,0:T(8,128)(2,1)S(1)}, bf16[2,2,2,2,32,1152]{5,4,3,2,1,0:T(8,128)(2,1)S(1)}, u32[]{:S(2)}, u32[]{:S(2)}) collective-permute-start(bf16[2,2,2,2,32,1152]{5,4,3,2,1,0:T(8,128)(2,1)S(1)} %dynamic-slice_bitcast_fusion.4), channel_id=1, source_target_pairs={{0,8},{8,0},{16,24},{24,16},{1,9},{9,1},{17,25},{25,17},{2,10},{10... | collective-permute-start | bytes 3538952 | tf_op jit(solution)/shard_map/ppermute | solution.py:146
  432.0 24.7 %collective-permute-start.41 = (bf16[2,2,32,1152]{3,2,1,0:T(8,128)(2,1)S(1)}, bf16[2,2,32,1152]{3,2,1,0:T(8,128)(2,1)S(1)}, u32[]{:S(2)}, u32[]{:S(2)}) collective-permute-start(bf16[2,2,32,1152]{3,2,1,0:T(8,128)(2,1)S(1)} %dynamic-slice_bitcast_fusion.16), channel_id=1, source_target_pairs={{0,4},{4,0},{1,5},{5,1},{2,6},{6,2},{3,7},{7,3},{8,12},{12,8},{9,1... | collective-permute-start | bytes 884744 | tf_op jit(solution)/shard_map/ppermute | solution.py:146
  464.3 46.2 %collective-permute-start.75 = (bf16[2,2,2,32,2624]{4,3,2,0,1:T(8,128)(2,1)S(1)}, bf16[2,2,2,32,2624]{4,3,2,0,1:T(8,128)(2,1)S(1)}, u32[]{:S(2)}, u32[]{:S(2)}) collective-permute-start(bf16[2,2,2,32,2624]{4,3,2,0,1:T(8,128)(2,1)S(1)} %dynamic-slice_bitcast_fusion.2), channel_id=1, source_target_pairs={{0,4},{4,0},{1,5},{5,1},{2,6},{6,2},{3,7},{7,3},{8,12},{12,8},{9,1... | collective-permute-start | bytes 4030472 | tf_op jit(solution)/shard_map/ppermute | solution.py:146
  468.1 45.4 %collective-permute-start.68 = (bf16[2,2,2,32,2624]{4,3,2,1,0:T(8,128)(2,1)S(1)}, bf16[2,2,2,32,2624]{4,3,2,1,0:T(8,128)(2,1)S(1)}, u32[]{:S(2)}, u32[]{:S(2)}) collective-permute-start(bf16[2,2,2,32,2624]{4,3,2,1,0:T(8,128)(2,1)S(1)} %dynamic-slice_bitcast_fusion.3), channel_id=1, source_target_pairs={{0,16},{8,24},{16,0},{24,8},{1,17},{9,25},{17,1},{25,9},{2,18},{10... | collective-permute-start | bytes 4030472 | tf_op jit(solution)/shard_map/ppermute | solution.py:146
  470.6 44.7 %collective-permute-start.82 = (bf16[2,2,2,32,2624]{4,3,0,2,1:T(8,128)(2,1)S(1)}, bf16[2,2,2,32,2624]{4,3,0,2,1:T(8,128)(2,1)S(1)}, u32[]{:S(2)}, u32[]{:S(2)}) collective-permute-start(bf16[2,2,2,32,2624]{4,3,0,2,1:T(8,128)(2,1)S(1)} %dynamic-slice_bitcast_fusion.1), channel_id=1, source_target_pairs={{0,1},{1,0},{2,3},{3,2},{4,5},{5,4},{6,7},{7,6},{8,9},{9,8},{10,11... | collective-permute-start | bytes 4030472 | tf_op jit(solution)/shard_map/ppermute | solution.py:146
  471.6 30.9 %collective-permute-start.43 = (bf16[32,1152]{1,0:T(8,128)(2,1)S(1)}, bf16[32,1152]{1,0:T(8,128)(2,1)S(1)}, u32[]{:S(2)}, u32[]{:S(2)}) collective-permute-start(bf16[32,1152]{1,0:T(8,128)(2,1)S(1)} %dynamic-slice_bitcast_fusion.28), channel_id=1, source_target_pairs={{0,2},{1,3},{2,0},{3,1},{4,6},{5,7},{6,4},{7,5},{8,10},{9,11},{10,... | collective-permute-start | bytes 221192 | tf_op jit(solution)/shard_map/ppermute | solution.py:146
  510.9 30.8 %collective-permute-start.76 = (bf16[2,2,32,2624]{3,2,1,0:T(8,128)(2,1)S(1)}, bf16[2,2,32,2624]{3,2,1,0:T(8,128)(2,1)S(1)}, u32[]{:S(2)}, u32[]{:S(2)}) collective-permute-start(bf16[2,2,32,2624]{3,2,1,0:T(8,128)(2,1)S(1)} %dynamic-slice_bitcast_fusion.7), channel_id=1, source_target_pairs={{0,1},{1,0},{2,3},{3,2},{4,5},{5,4},{6,7},{7,6},{8,9},{9,8},{10,11... | collective-permute-start | bytes 2015240 | tf_op jit(solution)/shard_map/ppermute | solution.py:146
  514.0 28.1 %collective-permute-start.69 = (bf16[2,2,32,2624]{3,2,1,0:T(8,128)(2,1)S(1)}, bf16[2,2,32,2624]{3,2,1,0:T(8,128)(2,1)S(1)}, u32[]{:S(2)}, u32[]{:S(2)}) collective-permute-start(bf16[2,2,32,2624]{3,2,1,0:T(8,128)(2,1)S(1)} %dynamic-slice_bitcast_fusion.8), channel_id=1, source_target_pairs={{0,4},{4,0},{1,5},{5,1},{2,6},{6,2},{3,7},{7,3},{8,12},{12,8},{9,1... | collective-permute-start | bytes 2015240 | tf_op jit(solution)/shard_map/ppermute | solution.py:146
  515.7 41.4 %collective-permute-start.83 = (bf16[2,2,32,2624]{3,2,0,1:T(8,128)(2,1)S(1)}, bf16[2,2,32,2624]{3,2,0,1:T(8,128)(2,1)S(1)}, u32[]{:S(2)}, u32[]{:S(2)}) collective-permute-start(bf16[2,2,32,2624]{3,2,0,1:T(8,128)(2,1)S(1)} %dynamic-slice_bitcast_fusion.6), channel_id=1, source_target_pairs={{0,2},{1,3},{2,0},{3,1},{4,6},{5,7},{6,4},{7,5},{8,10},{9,11},{10,... | collective-permute-start | bytes 2015240 | tf_op jit(solution)/shard_map/ppermute | solution.py:146
  542.0 21.2 %collective-permute-start.77 = (bf16[2,32,2624]{2,1,0:T(8,128)(2,1)S(1)}, bf16[2,32,2624]{2,1,0:T(8,128)(2,1)S(1)}, u32[]{:S(2)}, u32[]{:S(2)}) collective-permute-start(bf16[2,32,2624]{2,1,0:T(8,128)(2,1)S(1)} %dynamic-slice_bitcast_fusion.14), channel_id=1, source_target_pairs={{0,2},{1,3},{2,0},{3,1},{4,6},{5,7},{6,4},{7,5},{8,10},{9,11},{10,... | collective-permute-start | bytes 1007624 | tf_op jit(solution)/shard_map/ppermute | solution.py:146
  542.3 22.3 %collective-permute-start.70 = (bf16[2,32,2624]{2,1,0:T(8,128)(2,1)S(1)}, bf16[2,32,2624]{2,1,0:T(8,128)(2,1)S(1)}, u32[]{:S(2)}, u32[]{:S(2)}) collective-permute-start(bf16[2,32,2624]{2,1,0:T(8,128)(2,1)S(1)} %dynamic-slice_bitcast_fusion.15), channel_id=1, source_target_pairs={{0,1},{1,0},{2,3},{3,2},{4,5},{5,4},{6,7},{7,6},{8,9},{9,8},{10,11... | collective-permute-start | bytes 1007624 | tf_op jit(solution)/shard_map/ppermute | solution.py:146
  (114 other events, 831.2 us)
